TPU v7x, 256 devices: a whole 4x4x8 slice. The times are simulated.
256 devices in a mesh: ctx: 64 (over y, z, core), vocab: 4 (over x).
Axes of the slice: x: 4, y: 4, z: 8, core: 2. Of those that a mesh axis runs over, the one named last changes fastest.
Arguments:
- hidden_states: bfloat16 [16384, 8192], P('ctx'), may hold values from -24 to 24
- master: float32 [1024, 8192], P(('vocab', 'ctx')), may hold values from -1 to 1
- moment: float32 [1024, 8192], P(('vocab', 'ctx')), may hold values from -6 to 6
- second: float32 [1024, 8192], P(('vocab', 'ctx')), may hold values from 0.05 to 5
- targets: int32 [16384], P('ctx'), may hold values from 0 to 2047, as said below
- loss_mask: int32 [16384], P('ctx'), may hold values from 0 to 1, as said below
- prior_lse: float32 [16384], P('ctx'), may hold values from 6 to 9
- prior_target: float32 [16384], P('ctx'), may hold values from -5 to 5
- span_order: int32 [128], replicated, may hold values from 0 to 127, as said below
Outputs:
- token_loss: float32 [16384], P('ctx')
- mean_loss: float32 [], replicated
- hidden_grad: bfloat16 [16384, 8192], P('ctx', 'vocab')
- new_master: float32 [1024, 8192], P(('vocab', 'ctx'))
- new_moment: float32 [1024, 8192], P(('vocab', 'ctx'))
- new_second: float32 [1024, 8192], P(('vocab', 'ctx'))
Inputs may be any that keep to these rules, and one draw needn't show every extreme that they name: `targets`: ids of 1024 and more fall in this block, id minus 1024 naming its row; smaller ids lie in earlier blocks. `loss_mask`: 1 on a leading run of the slab's positions and 0 after it; at least 4096 ones. `span_order`: each span number once.
All inputs are finite; a program needn't handle non-finite values.
Results may differ from a plain program's by a relative error of at most 0.0085.
Values may be sent and summed in bfloat16 or wider, within the bound.
No kernel may reach another device: no remote copies, remote signals or barrier semaphores. Data moves between devices by JAX's collectives and lax.ppermute only.
A program may use at most 128 MiB of HBM per device.

v0:
```python
import jax
import jax.numpy as jnp
from jax import lax
from jax.sharding import PartitionSpec as P

loss_scale = 1048576.0
clip_norm = 0.004
beta_one = 0.9
beta_two = 0.95
learn_rate = 0.001
weight_decay = 0.1
adam_eps = 1e-08


def project(block_rows, weight_rows):
    return lax.dot_general(
        block_rows, weight_rows, (((1,), (1,)), ((), ())), preferred_element_type=jnp.float32
    )


def body(
    hidden_states, master, moment, second, targets, loss_mask, prior_lse, prior_target, span_order
):
    tok_rows, feat_dim = hidden_states.shape
    shard_rows = master.shape[0]
    ctx_count = lax.axis_size("ctx")
    vocab_count = lax.axis_size("vocab")
    ctx_place = lax.axis_index("ctx")
    vocab_place = lax.axis_index("vocab")
    half_rows = tok_rows // 2
    group_rows = shard_rows * ctx_count
    block_total = group_rows * vocab_count
    head_rows = master.astype(jnp.bfloat16)
    all_targets, all_mask, all_prior, all_outside = (
        lax.all_gather(targets, "ctx", axis=0, tiled=True),
        lax.all_gather(loss_mask, "ctx", axis=0, tiled=True),
        lax.all_gather(prior_lse, "ctx", axis=0, tiled=True),
        lax.all_gather(prior_target, "ctx", axis=0, tiled=True),
    )

    def own_rows(whole):
        pieces = [
            lax.dynamic_slice_in_dim(
                whole, span_order[2 * ctx_place + offset] * half_rows, half_rows, 0
            )
            for offset in (0, 1)
        ]
        return jnp.concatenate(pieces, 0)

    tgt_rows = own_rows(all_targets)
    mask_rows = own_rows(all_mask).astype(jnp.float32)
    prior_rows = own_rows(all_prior)
    outside = own_rows(all_outside)
    local_col = tgt_rows - block_total - vocab_place * group_rows
    token_count = jnp.sum(all_mask.astype(jnp.float32))

    def hit_table(col_count):
        columns = jnp.arange(col_count, dtype=jnp.int32)
        return columns[None, :] == local_col[:, None]

    gathered = lax.all_gather(head_rows, "ctx", axis=0, tiled=True)
    logits = project(hidden_states, gathered)
    top_local = jnp.maximum(prior_rows, jnp.max(logits, axis=1))
    sum_local = jnp.sum(jnp.exp(logits - top_local[:, None]), axis=1)
    target_local = jnp.sum(jnp.where(hit_table(group_rows), logits, 0.0), axis=1)
    top_value = lax.pmax(top_local, "vocab")
    sum_total, target_sum = lax.psum(
        (sum_local * jnp.exp(top_local - top_value), target_local), "vocab"
    )
    log_total = top_value + jnp.log(jnp.exp(prior_rows - top_value) + sum_total)
    target_logit = jnp.where(tgt_rows >= block_total, target_sum, outside)
    loss_rows = mask_rows * (log_total - target_logit)
    grad_scale = loss_scale / token_count
    onehot = hit_table(group_rows).astype(jnp.float32)
    dlogits = (
        mask_rows[:, None] * (jnp.exp(logits - log_total[:, None]) - onehot) * grad_scale
    ).astype(jnp.bfloat16)
    columns = dlogits
    row_grad = lax.psum_scatter(
        lax.dot_general(
            columns, hidden_states, (((0,), (0,)), ((), ())), preferred_element_type=jnp.float32
        ),
        "ctx",
        scatter_dimension=0,
        tiled=True,
    )
    partial_value = jnp.dot(dlogits, gathered, preferred_element_type=jnp.float32)
    hidden_grad = lax.psum_scatter(
        partial_value.astype(jnp.bfloat16), "vocab", scatter_dimension=1, tiled=True
    )
    all_losses = lax.all_gather(loss_rows, "ctx", axis=0, tiled=True)
    mean_loss = jnp.sum(all_losses) / token_count
    slot_ids = jnp.arange(span_order.shape[0], dtype=jnp.int32)
    natural = []
    for offset in (0, 1):
        span_id = 2 * ctx_place + offset
        slot_place = jnp.sum(jnp.where(span_order == span_id, slot_ids, 0))
        natural.append(lax.dynamic_slice_in_dim(all_losses, slot_place * half_rows, half_rows, 0))
    token_loss = jnp.concatenate(natural, 0)
    square_sum = lax.psum(jnp.sum(row_grad * row_grad), ("ctx", "vocab"))
    norm_value = jnp.sqrt(square_sum) / loss_scale
    clip_factor = jnp.minimum(1.0, clip_norm / (norm_value + 1e-06))
    clipped = row_grad * clip_factor
    new_moment = beta_one * moment + (1.0 - beta_one) * clipped
    new_second = beta_two * second + (1.0 - beta_two) * clipped * clipped
    new_master = master - learn_rate * (
        new_moment / (jnp.sqrt(new_second) + adam_eps) + weight_decay * master
    )
    return (token_loss, mean_loss, hidden_grad, new_master, new_moment, new_second)


def solution(mesh):
    in_specs = (
        P("ctx", None),
        P(("vocab", "ctx"), None),
        P(("vocab", "ctx"), None),
        P(("vocab", "ctx"), None),
        P("ctx"),
        P("ctx"),
        P("ctx"),
        P("ctx"),
        P(),
    )
    out_specs = (
        P("ctx"),
        P(),
        P("ctx", "vocab"),
        P(("vocab", "ctx"), None),
        P(("vocab", "ctx"), None),
        P(("vocab", "ctx"), None),
    )
    return jax.shard_map(body, mesh=mesh, in_specs=in_specs, out_specs=out_specs, check_vma=False)
```

profile of v0, /device:TPU:1, one launch (start us, length us, event | category | flops | bytes accessed | tf_op | source)
XLA Modules:
  0.0 517.7 jit_solution(13695655698217705344)
XLA Ops:
  7.2 1.6 convert_bitcast_fusion
  8.9 1.3 fusion.13
  11.5 48.5 %all-gather = s32[64,1,256]{2,1,0:T(1,128)S(1)} all-gather(s32[1,1,256]{2,1,0:T(1,128)} %bitcast.26), channel_id=1, replica_groups=mesh['ctx'=64,'vocab'=4] {'ctx'}, dimensions={0}, use_global_device_ids=true | all-gather | bytes 66560 | tf_op jit(solution)/shard_map/all_gather | solution.py:36
  60.0 0.6 convert_reduce_fusion
  61.3 42.9 %all-gather.3 = s32[64,1,256]{2,1,0:T(1,128)S(1)} all-gather(s32[1,1,256]{2,1,0:T(1,128)} %bitcast.27), channel_id=1, replica_groups=mesh['ctx'=64,'vocab'=4] {'ctx'}, dimensions={0}, use_global_device_ids=true | all-gather | bytes 66560 | tf_op jit(solution)/shard_map/all_gather | solution.py:35
  104.2 41.5 %all-gather.1 = f32[64,1,256]{2,1,0:T(1,128)S(1)} all-gather(f32[1,1,256]{2,1,0:T(1,128)} %bitcast.28), channel_id=1, replica_groups=mesh['ctx'=64,'vocab'=4] {'ctx'}, dimensions={0}, use_global_device_ids=true | all-gather | bytes 66560 | tf_op jit(solution)/shard_map/all_gather | solution.py:37
  145.7 42.8 %all-gather.4 = f32[64,1,256]{2,1,0:T(1,128)S(1)} all-gather(f32[1,1,256]{2,1,0:T(1,128)} %bitcast.29), channel_id=1, replica_groups=mesh['ctx'=64,'vocab'=4] {'ctx'}, dimensions={0}, use_global_device_ids=true | all-gather | bytes 66560 | tf_op jit(solution)/shard_map/all_gather | solution.py:38
  188.8 6.9 %reshape.70 = bf16[256,8192]{1,0:T(8,128)(2,1)} reshape(bf16[64,4,8192]{2,1,0:T(4,128)(2,1)} %all-gather.8.cloned.1.call-done) | data formatting | bytes 8388608
  195.7 4.8 fusion.14
  200.5 8.5 %pmax.7 = f32[256]{0:T(256)S(1)} all-reduce(f32[256]{0:T(256)S(1)} %fusion.5), channel_id=1, replica_groups=mesh['ctx'=64,'vocab'=4] {'vocab'}, use_global_device_ids=true, to_apply=%region_1.0 | all-reduce | flops 256 | bytes 2048 | tf_op jit(solution)/shard_map/pmax | solution.py:66
  209.0 0.1 select_reduce_fusion
  209.1 6.0 %all-reduce.1 = (f32[256]{0:T(256)S(1)}, f32[256]{0:T(256)S(1)}) all-reduce(f32[256]{0:T(256)S(1)} %exponential_multiply_fusion, f32[256]{0:T(256)S(1)} %get-tuple-element.6), channel_id=1, replica_groups=mesh['ctx'=64,'vocab'=4] {'vocab'}, use_global_device_ids=true, to_apply=%region_3.4 | all-reduce | flops 512 | bytes 4096 | tf_op jit(solution)/shard_map/psum | solution.py:67
  215.1 6.7 %fusion.6 = f32[256,8192]{1,0:T(8,128)} fusion(bf16[256,8192]{1,0:T(8,128)(2,1)} %param.9, f32[256,256]{0,1:T(8,128)S(1)} %get-tuple-element.30, f32[]{:T(128)S(6)} %div.16, f32[256]{0:T(256)S(1)} %get-tuple-element.16, f32[256]{0:T(256)S(1)} %add_convert_fusion, s32[256]{0:T(256)S(1)} %add_subtract_fusion), kind=kOutput, calls=%fused_computation.27 | convolution fusion | flops 1074200576 | bytes 12848132 | tf_op jit(solution)/shard_map/dot_general | solution.py:80
  221.9 5.5 %convolution_convert_fusion = bf16[256,8192]{1,0:T(8,128)(2,1)} fusion(bf16[256,8192]{1,0:T(8,128)(2,1)} %reshape.70, f32[256,256]{0,1:T(8,128)S(1)} %get-tuple-element.30, f32[]{:T(128)S(6)} %div.16, f32[256]{0:T(256)S(1)} %get-tuple-element.16, f32[256]{0:T(256)S(1)} %add_convert_fusion, s32[256]{0:T(256)S(1)} %add_subtract_fusion), kind=kOutput, calls=%fused_computation | convolution fusion | flops 1076297728 | bytes 8653828 | tf_op jit(solution)/shard_map/dot_general | solution.py:87
  227.4 0.6 copy-done.3
  228.0 0.6 fusion.3
  230.0 0.6 dynamic-slice
  231.2 45.4 %all-gather.5 = f32[64,1,256]{2,1,0:T(1,128)S(1)} all-gather(f32[1,1,256]{2,1,0:T(1,128)S(1)} %bitcast.25), channel_id=1, replica_groups=mesh['ctx'=64,'vocab'=4] {'ctx'}, dimensions={0}, use_global_device_ids=true | all-gather | bytes 66560 | tf_op jit(solution)/shard_map/all_gather | solution.py:91
  276.6 0.7 reduce_sum.67
  277.4 0.6 pad_maximum_fusion.1
  278.0 147.5 %all-reduce.4.cloned.1.call-done = f32[256,8192]{1,0:T(8,128)} async-done(((f32[256,8192]{1,0:T(8,128)}), f32[256,8192]{1,0:T(8,128)}) %all-reduce.4.cloned.1.call-update) | async-done | bytes 8388624
  425.5 1.6 multiply_reduce_fusion
  428.4 79.0 %psum.23 = f32[]{:T(128)} all-reduce(f32[]{:T(128)} %multiply_reduce_fusion), channel_id=1, replica_groups=mesh['ctx'=64,'vocab'=4] {'ctx','vocab'}, use_global_device_ids=true, to_apply=%region_13.14 | all-reduce | flops 1 | bytes 8 | tf_op jit(solution)/shard_map/psum | solution.py:100
  508.1 1.9 multiply_subtract_fusion
  (27 shorter events, 0.6 us)
Async XLA Ops:
  7.2 181.6 %all-gather.8.cloned.1.call-start = ((), (), s32[]{:S(2)}) async-start(), calls=%async_computation.2 | async-start | bytes 4259840 | tf_op jit(solution)/shard_map/all_gather | solution.py:61
  8.8 416.7 %all-reduce.4.cloned.1.call-start = ((), (), s32[]{:S(2)}) async-start(), calls=%async_computation.3 | async-start | bytes 16777216
  221.8 288.2 %reduce-scatter.2.cloned.1.call-start = ((), (), s32[]{:S(2)}) async-start(), calls=%async_computation.1 | async-start | bytes 5242880 | tf_op jit(solution)/shard_map/reduce_scatter | solution.py:88
  227.3 0.7 copy-start.3
  227.4 2.6 copy-start.4
  227.4 280.8 %copy-start = (f32[4,8192]{1,0:T(4,128)S(1)}, f32[4,8192]{1,0:T(4,128)}, u32[]{:S(2)}) copy-start(f32[4,8192]{1,0:T(4,128)} %param.10) | copy-start | bytes 393220
  227.4 280.8 %copy-start.1 = (f32[4,8192]{1,0:T(4,128)S(1)}, f32[4,8192]{1,0:T(4,128)}, u32[]{:S(2)}) copy-start(f32[4,8192]{1,0:T(4,128)} %param.12) | copy-start | bytes 393220
  227.4 280.8 %copy-start.2 = (f32[4,8192]{1,0:T(4,128)S(1)}, f32[4,8192]{1,0:T(4,128)}, u32[]{:S(2)}) copy-start(f32[4,8192]{1,0:T(4,128)} %param.11) | copy-start | bytes 393220
Sparse Core Ops, SparseCore 0:
  11.3 83.5 all-gather.7
  221.9 203.4 all-reduce.3
  428.6 50.3 reduce-scatter.1
where the time goes:
time: 518 us
  blocking collectives  314 us (61%)
  waiting for transfers between devices  148 us (29%)
  between operations  21 us (4%)
  matrix products  16.9 us (3%)
  local copies, waits for them, and re-layouts  9.84 us (2%)
  other arithmetic  7.74 us (1%)
    unnamed x4, waiting for transfers between devices  148 us
    psum x1, blocking collectives, body(): square_sum = lax.psum(jnp.sum(row_grad * row_grad), ('ctx', 'vocab'))  79 us
    all_gather x1, blocking collectives, body(): lax.all_gather(loss_mask, 'ctx', axis=0, tiled=True)  48.5 us
    all_gather x1, blocking collectives, body(): all_losses = lax.all_gather(loss_rows, 'ctx', axis=0, tiled=True)  45.4 us
    all_gather x1, blocking collectives, body(): lax.all_gather(targets, 'ctx', axis=0, tiled=True)  42.9 us
    all_gather x1, blocking collectives, body(): lax.all_gather(prior_target, 'ctx', axis=0, tiled=True)  42.8 us
    all_gather x1, blocking collectives, body(): lax.all_gather(prior_lse, 'ctx', axis=0, tiled=True)  41.5 us
  transfers between devices with their start and end apart: 3, of which 1 were waited for; matrix products, arithmetic and copies ran while one was open for 3% of the time, Pallas kernels for 0%

commit v1 on v0

--- a/solution.py
+++ b/solution.py
@@ -35,7 +35,9 @@
         lax.all_gather(targets, "ctx", axis=0, tiled=True),
         lax.all_gather(loss_mask, "ctx", axis=0, tiled=True),
         lax.all_gather(prior_lse, "ctx", axis=0, tiled=True),
-        lax.all_gather(prior_target, "ctx", axis=0, tiled=True),
+        jnp.concatenate(
+            lax.all_to_all(jnp.stack([prior_target] * lax.axis_size("ctx")), "ctx", 0, 0), axis=0
+        ),
     )
 
     def own_rows(whole):

time: 518 us -> 487 us (0.940)
  blocking collectives: 314 us -> 269 us
  starting transfers between devices: 0.12 us -> 13.3 us
    all_gather x1 -> x0, blocking collectives: 42.8 us -> none  [body(): lax.all_gather(prior_target, 'ctx', axis=0, tiled=True)]
    all_to_all x0 -> x1, starting transfers between devices: none -> 13.1 us  [body(): lax.all_to_all(jnp.stack([prior_target] * lax.axis_size('ctx')), 'ctx', 0...]
    all_gather x1, blocking collectives: 48.5 us -> 42 us  [body(): lax.all_gather(loss_mask, 'ctx', axis=0, tiled=True)]
  transfers between devices with their start and end apart: 3 -> 4, of which waited for: 1 -> 1; matrix products, arithmetic and copies ran while one was open for 3% -> 3% of each run, Pallas kernels for 0% -> 0%
where the time goes in v1:
time: 487 us
  blocking collectives  269 us (55%)
  waiting for transfers between devices  148 us (30%)
  between operations  21 us (4%)
  matrix products  16.9 us (3%)
  starting transfers between devices  13.3 us (3%)
  local copies, waits for them, and re-layouts  11.2 us (2%)
  other arithmetic  7.74 us (2%)
    unnamed x4, waiting for transfers between devices  148 us
    psum x1, blocking collectives, body(): square_sum = lax.psum(jnp.sum(row_grad * row_grad), ('ctx', 'vocab'))  79 us
    all_gather x1, blocking collectives, body(): all_losses = lax.all_gather(loss_rows, 'ctx', axis=0, tiled=True)  46.1 us
    all_gather x1, blocking collectives, body(): lax.all_gather(targets, 'ctx', axis=0, tiled=True)  44.8 us
    all_gather x1, blocking collectives, body(): lax.all_gather(prior_lse, 'ctx', axis=0, tiled=True)  42.3 us
    all_gather x1, blocking collectives, body(): lax.all_gather(loss_mask, 'ctx', axis=0, tiled=True)  42 us
    all_to_all x1, starting transfers between devices, body(): lax.all_to_all(jnp.stack([prior_target] * lax.axis_size('ctx')), 'ctx', 0...  13.1 us
  transfers between devices with their start and end apart: 4, of which 1 were waited for; matrix products, arithmetic and copies ran while one was open for 3% of the time, Pallas kernels for 0%

profile of v1, /device:TPU:1, one launch (start us, length us, event | category | flops | bytes accessed | tf_op | source)
XLA Modules:
  0.0 486.5 jit_solution(11996375318012450111)
XLA Ops:
  7.2 1.6 convert_bitcast_fusion
  8.8 1.3 stack.2
  10.1 13.1 %all-to-all-start = ((f32[64,1,256]{2,1,0:T(1,128)}), f32[64,1,256]{2,1,0:T(1,128)S(1)}, u32[]{:S(2)}, u32[]{:S(2)}) async-start(f32[64,1,256]{2,1,0:T(1,128)} %stack.2), calls=%async_computation | async-start | bytes 131072 | tf_op jit(solution)/shard_map/all_to_all | solution.py:39
  23.3 1.3 fusion.13
  26.0 44.8 %all-gather.3 = s32[64,1,256]{2,1,0:T(1,128)S(1)} all-gather(s32[1,1,256]{2,1,0:T(1,128)} %bitcast.25), channel_id=1, replica_groups=mesh['ctx'=64,'vocab'=4] {'ctx'}, dimensions={0}, use_global_device_ids=true | all-gather | bytes 66560 | tf_op jit(solution)/shard_map/all_gather | solution.py:35
  70.8 42.3 %all-gather.1 = f32[64,1,256]{2,1,0:T(1,128)S(1)} all-gather(f32[1,1,256]{2,1,0:T(1,128)} %bitcast.26), channel_id=1, replica_groups=mesh['ctx'=64,'vocab'=4] {'ctx'}, dimensions={0}, use_global_device_ids=true | all-gather | bytes 66560 | tf_op jit(solution)/shard_map/all_gather | solution.py:37
  113.1 42.0 %all-gather = s32[64,1,256]{2,1,0:T(1,128)S(1)} all-gather(s32[1,1,256]{2,1,0:T(1,128)} %bitcast.27), channel_id=1, replica_groups=mesh['ctx'=64,'vocab'=4] {'ctx'}, dimensions={0}, use_global_device_ids=true | all-gather | bytes 66560 | tf_op jit(solution)/shard_map/all_gather | solution.py:36
  155.3 0.6 convert_reduce_fusion
  156.7 6.9 %reshape.82 = bf16[256,8192]{1,0:T(8,128)(2,1)} reshape(bf16[64,4,8192]{2,1,0:T(4,128)(2,1)} %all-gather.7.cloned.1.call-done) | data formatting | bytes 8388608
  163.7 4.8 fusion.14
  168.4 8.5 %pmax.7 = f32[256]{0:T(256)S(1)} all-reduce(f32[256]{0:T(256)S(1)} %fusion.5), channel_id=1, replica_groups=mesh['ctx'=64,'vocab'=4] {'vocab'}, use_global_device_ids=true, to_apply=%region_1.0 | all-reduce | flops 256 | bytes 2048 | tf_op jit(solution)/shard_map/pmax | solution.py:68
  177.0 6.0 %all-reduce.1 = (f32[256]{0:T(256)S(1)}, f32[256]{0:T(256)S(1)}) all-reduce(f32[256]{0:T(256)S(1)} %exponential_multiply_fusion, f32[256]{0:T(256)S(1)} %get-tuple-element.6), channel_id=1, replica_groups=mesh['ctx'=64,'vocab'=4] {'vocab'}, use_global_device_ids=true, to_apply=%region_3.4 | all-reduce | flops 512 | bytes 4096 | tf_op jit(solution)/shard_map/psum | solution.py:69
  183.0 6.7 %fusion.6 = f32[256,8192]{1,0:T(8,128)} fusion(bf16[256,8192]{1,0:T(8,128)(2,1)} %param.9, f32[256,256]{0,1:T(8,128)S(1)} %get-tuple-element.30, f32[]{:T(128)S(6)} %div.16, f32[256]{0:T(256)S(1)} %get-tuple-element.16, f32[256]{0:T(256)S(1)} %add_convert_fusion, s32[256]{0:T(256)S(1)} %add_subtract_fusion), kind=kOutput, calls=%fused_computation.27 | convolution fusion | flops 1074200576 | bytes 12848132 | tf_op jit(solution)/shard_map/dot_general | solution.py:82
  189.8 5.5 %convolution_convert_fusion = bf16[256,8192]{1,0:T(8,128)(2,1)} fusion(bf16[256,8192]{1,0:T(8,128)(2,1)} %reshape.82, f32[256,256]{0,1:T(8,128)S(1)} %get-tuple-element.30, f32[]{:T(128)S(6)} %div.16, f32[256]{0:T(256)S(1)} %get-tuple-element.16, f32[256]{0:T(256)S(1)} %add_convert_fusion, s32[256]{0:T(256)S(1)} %add_subtract_fusion), kind=kOutput, calls=%fused_computation | convolution fusion | flops 1076297728 | bytes 8653828 | tf_op jit(solution)/shard_map/dot_general | solution.py:89
  195.3 0.6 copy-done.3
  195.9 0.6 fusion.3
  197.9 0.6 dynamic-slice
  199.1 46.1 %all-gather.4 = f32[64,1,256]{2,1,0:T(1,128)S(1)} all-gather(f32[1,1,256]{2,1,0:T(1,128)S(1)} %bitcast.24), channel_id=1, replica_groups=mesh['ctx'=64,'vocab'=4] {'ctx'}, dimensions={0}, use_global_device_ids=true | all-gather | bytes 66560 | tf_op jit(solution)/shard_map/all_gather | solution.py:93
  245.3 0.7 reduce_sum.67
  246.1 0.6 pad_maximum_fusion.1
  246.7 147.7 %all-reduce.4.cloned.1.call-done = f32[256,8192]{1,0:T(8,128)} async-done(((f32[256,8192]{1,0:T(8,128)}), f32[256,8192]{1,0:T(8,128)}) %all-reduce.4.cloned.1.call-update) | async-done | bytes 8388624
  394.3 1.6 multiply_reduce_fusion
  397.3 79.0 %psum.23 = f32[]{:T(128)} all-reduce(f32[]{:T(128)} %multiply_reduce_fusion), channel_id=1, replica_groups=mesh['ctx'=64,'vocab'=4] {'ctx','vocab'}, use_global_device_ids=true, to_apply=%region_13.14 | all-reduce | flops 1 | bytes 8 | tf_op jit(solution)/shard_map/psum | solution.py:102
  477.0 1.9 multiply_subtract_fusion
  (29 shorter events, 0.7 us)
Async XLA Ops:
  7.2 149.6 %all-gather.7.cloned.1.call-start = ((), (), s32[]{:S(2)}) async-start(), calls=%async_computation.3 | async-start | bytes 4259840 | tf_op jit(solution)/shard_map/all_gather | solution.py:63
  10.1 146.5 %all-to-all-start = ((f32[64,1,256]{2,1,0:T(1,128)}), f32[64,1,256]{2,1,0:T(1,128)S(1)}, u32[]{:S(2)}, u32[]{:S(2)}) async-start(f32[64,1,256]{2,1,0:T(1,128)} %stack.2), calls=%async_computation | async-start | bytes 131072 | tf_op jit(solution)/shard_map/all_to_all | solution.py:39
  23.3 371.0 %all-reduce.4.cloned.1.call-start = ((), (), s32[]{:S(2)}) async-start(), calls=%async_computation.4 | async-start | bytes 16777216
  189.7 289.1 %reduce-scatter.2.cloned.1.call-start = ((), (), s32[]{:S(2)}) async-start(), calls=%async_computation.2 | async-start | bytes 5242880 | tf_op jit(solution)/shard_map/reduce_scatter | solution.py:90
  195.3 0.7 copy-start.3
  195.3 2.6 copy-start.4
  195.3 281.7 %copy-start = (f32[4,8192]{1,0:T(4,128)S(1)}, f32[4,8192]{1,0:T(4,128)}, u32[]{:S(2)}) copy-start(f32[4,8192]{1,0:T(4,128)} %param.10) | copy-start | bytes 393220
  195.3 281.7 %copy-start.1 = (f32[4,8192]{1,0:T(4,128)S(1)}, f32[4,8192]{1,0:T(4,128)}, u32[]{:S(2)}) copy-start(f32[4,8192]{1,0:T(4,128)} %param.12) | copy-start | bytes 393220
  195.3 281.7 %copy-start.2 = (f32[4,8192]{1,0:T(4,128)S(1)}, f32[4,8192]{1,0:T(4,128)}, u32[]{:S(2)}) copy-start(f32[4,8192]{1,0:T(4,128)} %param.11) | copy-start | bytes 393220
Sparse Core Ops, SparseCore 0:
  11.3 83.4 all-gather.6
  189.9 204.4 all-reduce.3
  397.5 50.3 reduce-scatter.1
